TPU v7x, 32 devices: a whole 2x2x4 slice. The times are simulated.
32 devices in a mesh: head: 4 (over z), seq: 8 (over y, x, core).
Axes of the slice: x: 2, y: 2, z: 4, core: 2. Of those that a mesh axis runs over, the one named last changes fastest.
Arguments:
- keys: bfloat16 [2, 4096, 2560], P(None, 'seq', 'head'), may hold values from -6 to 6
- values: bfloat16 [2, 4096, 2560], P(None, 'seq', 'head'), may hold values from -6 to 6
- step_rates: float32 [2, 4, 4096], P(None, 'head', 'seq'), may hold values from 0.05 to 1
- queries: bfloat16 [4096, 2560], P('seq', 'head'), may hold values from -6 to 6
- first_weight: bfloat16 [4, 640, 640], P('head'), may hold values from -0.25 to 0.25
- third_weight: bfloat16 [4, 640, 640], P('head'), may hold values from -0.25 to 0.25
- second_weight: bfloat16 [4, 640, 640], P('head'), may hold values from -0.25 to 0.25
- out_weight: bfloat16 [2560, 2560], P('head'), may hold values from -0.125 to 0.125
- live_counts: int32 [3, 8], P(None, 'seq'), may hold values from 256 to 512
Outputs:
- mixed: bfloat16 [4096, 2560], P('seq', 'head')
Inputs may be any that keep to these rules, and one draw needn't show every extreme that they name: `live_counts`: the live rows of a shard are its first ones.
All inputs are finite; a program needn't handle non-finite values.
Results may differ from a plain program's by a relative error of at most 0.023.
Values may be sent and summed in bfloat16 or wider, within the bound.
A program may use at most 128 MiB of HBM per device.

v0:
```python
import jax
import jax.numpy as jnp
from jax import lax
from jax.sharding import PartitionSpec as P

NS_ITERS = 3


coef_a = 3.4445
coef_b = -4.775
coef_c = 2.0315
step_size = 0.5


def contract_rows(left, right):
    return lax.dot_general(
        left, right, (((0,), (0,)), ((), ())), preferred_element_type=jnp.float32
    )


def contract_cols(left, right):
    return lax.dot_general(
        left, right, (((1,), (1,)), ((), ())), preferred_element_type=jnp.float32
    )


def fast_grads(inputs, targets, scaling, first, third, second):
    first_pre = jnp.dot(inputs, first, preferred_element_type=jnp.float32)
    third_pre = jnp.dot(inputs, third, preferred_element_type=jnp.float32)
    sigmoid = jax.nn.sigmoid(first_pre)
    swish = first_pre * sigmoid
    hidden = (swish * third_pre).astype(jnp.bfloat16)
    weighted = (targets.astype(jnp.float32) * scaling[:, None]).astype(jnp.bfloat16)
    grad_second = contract_rows(hidden, weighted)
    back = contract_cols(weighted, second)
    back_first = (back * third_pre * sigmoid * (1.0 + first_pre * (1.0 - sigmoid))).astype(
        jnp.bfloat16
    )
    back_third = (back * swish).astype(jnp.bfloat16)
    return (contract_rows(inputs, back_first), contract_rows(inputs, back_third), grad_second)


def poly_step(current, gram_wide):
    gram_low = gram_wide.astype(jnp.bfloat16)
    poly = (
        coef_b * gram_wide
        + coef_c * jnp.dot(gram_low, gram_low, preferred_element_type=jnp.float32)
    ).astype(jnp.bfloat16)
    return (
        coef_a * current.astype(jnp.float32)
        + jnp.dot(poly, current, preferred_element_type=jnp.float32)
    ).astype(jnp.bfloat16)


def orthogonal(gradient):
    scale = jnp.sqrt(jnp.sum(gradient * gradient)) + 1e-06
    current = (gradient / scale).astype(jnp.bfloat16)
    for index in range(NS_ITERS):
        current = poly_step(current, contract_cols(current, current))
    return current


def rescaled(weight, ortho):
    old = weight.astype(jnp.float32)
    fresh = old + step_size * ortho.astype(jnp.float32)
    ratio = jnp.sqrt(jnp.mean(old * old, axis=0) + 1e-06) / jnp.sqrt(
        jnp.mean(fresh * fresh, axis=0) + 1e-06
    )
    return (fresh * ratio[None, :]).astype(jnp.bfloat16)


def on_device(
    keys,
    values,
    step_rates,
    queries,
    first_weight,
    third_weight,
    second_weight,
    out_weight,
    live_counts,
):
    group_count = keys.shape[0]
    rows = keys.shape[1]
    positions = jnp.arange(rows, dtype=jnp.int32)
    first = first_weight[0]
    third = third_weight[0]
    second = second_weight[0]
    totals = None
    for group in range(group_count):
        live = (positions < live_counts[group, 0]).astype(jnp.float32)
        scaling = live * step_rates[group, 0]
        parts = fast_grads(keys[group], values[group], scaling, first, third, second)
        totals = parts if totals is None else tuple((a + b for a, b in zip(totals, parts)))
    totals = lax.psum(totals, "seq")
    new_first = rescaled(first, orthogonal(totals[0]))
    new_third = rescaled(third, orthogonal(totals[1]))
    new_second = rescaled(second, orthogonal(totals[2]))
    live_query = (positions < live_counts[group_count, 0]).astype(jnp.float32)
    first_pre = jnp.dot(queries, new_first, preferred_element_type=jnp.float32)
    third_pre = jnp.dot(queries, new_third, preferred_element_type=jnp.float32)
    hidden = (jax.nn.silu(first_pre) * third_pre).astype(jnp.bfloat16)
    head_out = (
        jnp.dot(hidden, new_second, preferred_element_type=jnp.float32) * live_query[:, None]
    ).astype(jnp.bfloat16)
    columns = lax.all_to_all(out_weight, "head", split_axis=1, concat_axis=0, tiled=True)
    mixed = jnp.dot(
        lax.all_gather(head_out, "head", axis=1, tiled=True),
        columns,
        preferred_element_type=jnp.float32,
    )
    return mixed.astype(jnp.bfloat16)


def solution(mesh):
    in_specs = (
        P(None, "seq", "head"),
        P(None, "seq", "head"),
        P(None, "head", "seq"),
        P("seq", "head"),
        P("head", None, None),
        P("head", None, None),
        P("head", None, None),
        P("head", None),
        P(None, "seq"),
    )
    out_specs = P("seq", "head")
    return jax.shard_map(
        on_device, mesh=mesh, in_specs=in_specs, out_specs=out_specs, check_vma=False
    )
```

profile of v0, /device:TPU:0, one launch (start us, length us, event | category | flops | bytes accessed | tf_op | source)
XLA Modules:
  0.0 265.2 jit_solution(14986200987630402233)
XLA Ops:
  6.5 2.2 fusion.16
  8.8 0.7 fusion.14
  10.0 0.7 fusion.20
  10.8 0.7 fusion.18
  11.5 0.7 fusion.147
  12.2 0.6 fusion.112
  12.8 0.8 fusion.24
  13.7 0.8 fusion.73
  14.4 1.0 fusion.86
  15.4 0.9 fusion.74
  16.4 0.6 fusion.113
  17.0 0.8 fusion.22
  17.8 1.9 add_bitcast_fusion
  19.8 2.2 add_bitcast_fusion.1
  22.0 2.1 convolution_add_fusion
  24.1 5.7 %copy.56 = bf16[640,2560]{0,1:T(8,128)(2,1)} copy(bf16[640,2560]{1,0:T(8,128)(2,1)} %param.16) | data formatting | bytes 6553600 | tf_op args[7]
  29.8 6.4 %all-to-all-start = ((bf16[640,4,640]{0,2,1:T(8,128)(2,1)}), bf16[640,4,640]{0,2,1:T(8,128)(2,1)}, u32[]{:S(2)}, u32[]{:S(2)}) async-start(bf16[640,4,640]{0,2,1:T(8,128)(2,1)} %bitcast.122), calls=%async_computation | async-start | bytes 6553600 | tf_op jit(solution)/shard_map/all_to_all | solution.py:106
  36.1 1.3 copy.42
  37.4 1.3 copy.41
  38.7 1.3 copy.40
  40.0 0.6 fusion.114
  40.6 75.4 %all-reduce.3.cloned.1.call-done = (f32[640,640]{0,1:T(8,128)}, f32[640,640]{0,1:T(8,128)}, f32[640,640]{0,1:T(8,128)}) async-done(((f32[640,640]{0,1:T(8,128)}, f32[640,640]{0,1:T(8,128)}, f32[640,640]{0,1:T(8,128)}), (f32[640,640]{0,1:T(8,128)}, f32[640,640]{0,1:T(8,128)}, f32[640,640]{0,1:T(8,128)})) %all-reduce.3.cloned.1.call-update) | async-done | bytes 4915216 | tf_op jit(solution)/shard_map/psum | solution.py:95
  116.0 3.1 %multiply_reduce_fusion.1 = (f32[]{:T(128)}, f32[]{:T(128)}) fusion(f32[640,640]{0,1:T(8,128)} %get-tuple-element.13, f32[640,640]{0,1:T(8,128)} %get-tuple-element.12), kind=kLoop, calls=%fused_computation.18 | loop fusion | flops 1638398 | bytes 3276808 | tf_op jit(solution)/shard_map/reduce_sum | solution.py:56
  119.8 2.1 fusion.144
  121.9 5.1 %add_convert_fusion.10 = bf16[640,640]{0,1:T(8,128)(2,1)S(1)} fusion(f32[640,640]{1,0:T(8,128)} %fusion.144, f32[640,640]{0,1:T(8,128)} %get-tuple-element.12, f32[]{:T(128)S(6)} %add.170), kind=kOutput, calls=%fused_computation.25 | convolution fusion | flops 1053900800 | bytes 4096004 | tf_op jit(solution)/shard_map/dot_general | solution.py:51
  127.0 2.1 fusion.156
  129.1 4.4 %add_convert_fusion.8 = bf16[640,640]{0,1:T(8,128)(2,1)S(1)} fusion(bf16[640,640]{0,1:T(8,128)(2,1)S(1)} %add_convert_fusion.10, f32[640,640]{1,0:T(8,128)} %fusion.156), kind=kOutput, calls=%fused_computation.23 | convolution fusion | flops 1052262400 | bytes 3276800 | tf_op jit(solution)/shard_map/dot_general | solution.py:51
  133.5 2.1 fusion.157
  136.2 2.1 fusion.145
  138.4 5.0 %add_convert_fusion.4 = bf16[640,640]{0,1:T(8,128)(2,1)S(1)} fusion(f32[640,640]{1,0:T(8,128)} %fusion.145, f32[640,640]{0,1:T(8,128)} %get-tuple-element.13, f32[]{:T(128)S(6)} %add.181), kind=kOutput, calls=%fused_computation.15 | convolution fusion | flops 1053900800 | bytes 4096004 | tf_op jit(solution)/shard_map/dot_general | solution.py:51
  143.4 2.2 fusion.158
  145.6 4.4 %add_convert_fusion.2 = bf16[640,640]{0,1:T(8,128)(2,1)S(1)} fusion(bf16[640,640]{0,1:T(8,128)(2,1)S(1)} %add_convert_fusion.4, f32[640,640]{1,0:T(8,128)} %fusion.158), kind=kOutput, calls=%fused_computation.13 | convolution fusion | flops 1052262400 | bytes 3276800 | tf_op jit(solution)/shard_map/dot_general | solution.py:51
  150.0 2.2 fusion.159
  152.2 1.0 multiply_reduce_fusion.5
  153.9 4.2 %fusion.143 = f32[640,640]{1,0:T(8,128)} fusion(f32[640,640]{0,1:T(8,128)} %get-tuple-element.11, f32[]{:T(128)S(6)} %add.157), kind=kOutput, calls=%fused_computation.183 | convolution fusion | flops 525107200 | bytes 3276804 | tf_op jit(solution)/shard_map/dot_general | solution.py:22
  158.1 5.4 %add_convert_fusion.16 = bf16[640,640]{0,1:T(8,128)(2,1)S(1)} fusion(f32[640,640]{1,0:T(8,128)} %fusion.143, f32[640,640]{0,1:T(8,128)} %get-tuple-element.11, f32[]{:T(128)S(6)} %add.157), kind=kOutput, calls=%fused_computation.36 | convolution fusion | flops 1053900800 | bytes 4096004 | tf_op jit(solution)/shard_map/dot_general | solution.py:51
  163.6 0.9 copy-done.5
  164.4 2.1 fusion.154
  166.5 4.8 %add_convert_fusion.14 = bf16[640,640]{0,1:T(8,128)(2,1)S(1)} fusion(bf16[640,640]{0,1:T(8,128)(2,1)} %copy-done.5, f32[640,640]{1,0:T(8,128)} %fusion.154), kind=kOutput, calls=%fused_computation.34 | convolution fusion | flops 1052262400 | bytes 3276800 | tf_op jit(solution)/shard_map/dot_general | solution.py:51
  171.3 2.1 fusion.155
  173.4 5.6 %fusion.1 = (f32[640]{0:T(1024)S(1)}, f32[640]{0:T(1024)S(1)}, bf16[640,640]{0,1:T(8,128)(2,1)}) fusion(bf16[1,640,640]{1,2,0:T(8,128)(2,1)} %copy.42, bf16[640,640]{0,1:T(8,128)(2,1)S(1)} %add_convert_fusion.8, f32[640,640]{1,0:T(8,128)} %fusion.157), kind=kOutput, calls=%fused_computation.7 | convolution fusion | flops 1055537920 | bytes 4101120 | tf_op jit(solution)/shard_map/dot_general | solution.py:51
  179.0 5.6 %fusion.2 = (f32[640]{0:T(1024)S(1)}, f32[640]{0:T(1024)S(1)}, bf16[640,640]{0,1:T(8,128)(2,1)}) fusion(bf16[1,640,640]{1,2,0:T(8,128)(2,1)} %copy.41, bf16[640,640]{0,1:T(8,128)(2,1)S(1)} %add_convert_fusion.2, f32[640,640]{1,0:T(8,128)} %fusion.159), kind=kOutput, calls=%fused_computation.8 | convolution fusion | flops 1055537920 | bytes 4101120 | tf_op jit(solution)/shard_map/dot_general | solution.py:51
  184.6 5.5 %fusion = (f32[640]{0:T(1024)S(1)}, f32[640]{0:T(1024)S(1)}, bf16[640,640]{0,1:T(8,128)(2,1)}) fusion(bf16[1,640,640]{1,2,0:T(8,128)(2,1)S(1)} %copy-done.12, bf16[640,640]{0,1:T(8,128)(2,1)S(1)} %add_convert_fusion.14, f32[640,640]{1,0:T(8,128)} %fusion.155), kind=kOutput, calls=%fused_computation.6 | convolution fusion | flops 1055537920 | bytes 4101120 | tf_op jit(solution)/shard_map/dot_general | solution.py:51
  190.2 3.4 %convolution_bitcast_fusion.1 = f32[512,640]{1,0:T(8,128)} fusion(bf16[512,640]{1,0:T(8,128)(2,1)S(1)} %copy-done, bf16[640,640]{0,1:T(8,128)(2,1)} %get-tuple-element.19, bf16[1,640,640]{1,2,0:T(8,128)(2,1)} %copy.40, f32[640]{0:T(1024)S(1)} %rsqrt_multiply_fusion.2), kind=kOutput, calls=%fused_computation.49 | convolution fusion | flops 421888000 | bytes 3607040 | tf_op jit(solution)/shard_map/dot_general | solution.py:100
  193.6 4.2 %fusion.5 = bf16[512,640]{1,0:T(8,128)(2,1)} fusion(bf16[512,640]{1,0:T(8,128)(2,1)S(1)} %copy-done, f32[512,640]{1,0:T(8,128)} %convolution_bitcast_fusion.1, bf16[640,640]{0,1:T(8,128)(2,1)} %get-tuple-element.21, bf16[640,640]{0,1:T(8,128)(2,1)} %get-tuple-element.20, bf16[1,640,640]{1,2,0:T(8,128)(2,1)S(1)} %copy-done.10, ...), kind=kOutput, calls=%fused_computation.51 | convolution fusion | flops 846397440 | bytes 5905408 | tf_op jit(solution)/shard_map/dot_general | solution.py:104
  197.8 5.7 %copy.57 = bf16[4,640,640]{2,1,0:T(8,128)(2,1)} copy(bf16[4,640,640]{1,2,0:T(8,128)(2,1)} %bitcast.19) | data formatting | bytes 6553600 | tf_op jit(solution)/shard_map/all_to_all | solution.py:106
  203.5 49.1 %all-gather.2.cloned.1.call-done = bf16[512,2560]{1,0:T(8,128)(2,1)} async-done(((bf16[512,640]{1,0:T(8,128)(2,1)}), bf16[512,2560]{1,0:T(8,128)(2,1)}) %all-gather.2.cloned.1.call-update) | async-done | bytes 2621456 | tf_op jit(solution)/shard_map/all_gather | solution.py:108
  252.6 5.7 %convolution_convert_fusion = bf16[512,640]{1,0:T(8,128)(2,1)} fusion(bf16[512,2560]{1,0:T(8,128)(2,1)} %all-gather.2.cloned.1.call-done, bf16[2560,640]{1,0:T(8,128)(2,1)} %bitcast.123), kind=kOutput, calls=%fused_computation.52 | convolution fusion | flops 1678049280 | bytes 6553600 | tf_op jit(solution)/shard_map/dot_general | solution.py:107
  (38 shorter events, 0.5 us)
Async XLA Ops:
  6.5 183.6 %copy-start = (bf16[512,640]{1,0:T(8,128)(2,1)S(1)}, bf16[512,640]{1,0:T(8,128)(2,1)}, u32[]{:S(2)}) copy-start(bf16[512,640]{1,0:T(8,128)(2,1)} %param.12) | copy-start | bytes 1966084
  6.5 2.3 copy-start.3
  6.5 109.5 %all-reduce.3.cloned.1.call-start = ((), (), s32[]{:S(2)}) async-start(), calls=%async_computation.2 | async-start | bytes 9830400 | tf_op jit(solution)/shard_map/psum | solution.py:95
  6.5 2.3 copy-start.4
  8.8 1.1 copy-start.1
  10.7 0.8 copy-start.13
  10.7 1.5 copy-start.14
  10.7 2.1 copy-start.2
  10.8 2.1 copy-start.9
  29.8 168.1 %all-to-all-start = ((bf16[640,4,640]{0,2,1:T(8,128)(2,1)}), bf16[640,4,640]{0,2,1:T(8,128)(2,1)}, u32[]{:S(2)}, u32[]{:S(2)}) async-start(bf16[640,4,640]{0,2,1:T(8,128)(2,1)} %bitcast.122), calls=%async_computation | async-start | bytes 6553600 | tf_op jit(solution)/shard_map/all_to_all | solution.py:106
  36.1 216.5 %all-gather.2.cloned.1.call-start = ((), (), s32[]{:S(2)}) async-start(), calls=%async_computation.1 | async-start | bytes 3276800 | tf_op jit(solution)/shard_map/all_gather | solution.py:108
  116.0 3.8 %copy-start.8 = (f32[640,640]{0,1:T(8,128)S(1)}, f32[640,640]{0,1:T(8,128)}, u32[]{:S(2)}) copy-start(f32[640,640]{0,1:T(8,128)} %get-tuple-element.12) | copy-start | bytes 4915204
  133.4 2.8 %copy-start.7 = (f32[640,640]{0,1:T(8,128)S(1)}, f32[640,640]{0,1:T(8,128)}, u32[]{:S(2)}) copy-start(f32[640,640]{0,1:T(8,128)} %get-tuple-element.13) | copy-start | bytes 4915204
  150.0 2.2 copy-start.6
  163.5 0.9 copy-start.5
  179.0 5.6 %copy-start.12 = (bf16[1,640,640]{1,2,0:T(8,128)(2,1)S(1)}, bf16[1,640,640]{1,2,0:T(8,128)(2,1)}, u32[]{:S(2)}) copy-start(bf16[1,640,640]{1,2,0:T(8,128)(2,1)} %copy.40) | copy-start | bytes 2457604
  190.2 3.5 %copy-start.10 = (bf16[1,640,640]{1,2,0:T(8,128)(2,1)S(1)}, bf16[1,640,640]{1,2,0:T(8,128)(2,1)}, u32[]{:S(2)}) copy-start(bf16[1,640,640]{1,2,0:T(8,128)(2,1)} %copy.42) | copy-start | bytes 2457604
  190.2 3.5 %copy-start.11 = (bf16[1,640,640]{1,2,0:T(8,128)(2,1)S(1)}, bf16[1,640,640]{1,2,0:T(8,128)(2,1)}, u32[]{:S(2)}) copy-start(bf16[1,640,640]{1,2,0:T(8,128)(2,1)} %copy.41) | copy-start | bytes 2457604
Sparse Core Ops, SparseCore 0:
  24.2 91.7 all-reduce.2
  197.9 54.6 all-gather.1
where the time goes:
time: 266 us; the launch traced here: 265 us
  waiting for transfers between devices  125 us (47%)
  matrix products  95.3 us (36%)
  local copies, waits for them, and re-layouts  17.2 us (6%)
  between operations  15.8 us (6%)
  starting transfers between devices  6.37 us (2%)
  other arithmetic  6.05 us (2%)
    psum x1, waiting for transfers between devices, on_device(): totals = lax.psum(totals, 'seq')  75.4 us
    all_gather x1, waiting for transfers between devices, on_device(): lax.all_gather(head_out, 'head', axis=1, tiled=True)  49.1 us
    dot_general x9, matrix products, poly_step(): jnp.dot(poly, current, preferred_element_type=jnp.float32)  45.8 us
    dot_general x11, matrix products, contract_cols(): lax.dot_general(left, right, (((1,), (1,)), ((), ())), preferred_element_...  22.8 us
    unnamed x34, local copies, waits for them, and re-layouts  10.9 us
    dot_general x6, matrix products, contract_rows(): lax.dot_general(left, right, (((0,), (0,)), ((), ())), preferred_element_...  8.9 us
    all_to_all x1, starting transfers between devices, on_device(): lax.all_to_all(out_weight, 'head', split_axis=1, concat_axis=0, tiled=True)  6.36 us
    dot_general x1, matrix products, on_device(): jnp.dot(lax.all_gather(head_out, 'head', axis=1, tiled=True), columns, pr...  5.75 us
  transfers between devices with their start and end apart: 3, of which 2 were waited for; matrix products, arithmetic and copies ran while one was open for 36% of the time, Pallas kernels for 0%

commit v1 on v0

v1 whole, which is shorter than its diff:
```python
import functools

import jax
import jax.numpy as jnp
from jax import lax
from jax.experimental import pallas as pl
from jax.experimental.pallas import tpu as pltpu
from jax.sharding import PartitionSpec as P

NS_ITERS = 3
coef_a = 3.4445
coef_b = -4.775
coef_c = 2.0315
step_size = 0.5

MESH = pl.DeviceIdType.MESH
F32 = jnp.float32
BF16 = jnp.bfloat16


def dot(left, right, dims=((1,), (0,))):
    return lax.dot_general(left, right, (dims, ((), ())), preferred_element_type=F32)


def kernel(
    heads, shards, tile,
    keys, values, scaling, queries, live_query, first, third, second, out_weight,
    mixed,
    gate_s, swish_s, hidden_s, weighted_s, back_first_s, back_third_s,
    wide, gram_s, current, poly_s, fresh_w,
    send_a, recv_a, send_b, recv_b, full, columns, head_out,
    ag_right, ag_left, rs_right, rs_left, rs_send_right, rs_send_left, total_ag,
    sem_a, sem_b, sem_c, sem_d, sem_w, sem_x, sem_ag, sem_rs,
):
    chips = shards // 2
    rows, width = keys.shape
    grad_rows = width // shards
    z = lax.axis_index("head")
    s = lax.axis_index("seq")
    core = lax.rem(s, 2)
    chip = s // 2
    partner = {"seq": s + 1 - 2 * core}
    half = width // 2
    tokens = queries.shape[0]
    part = tokens // 2

    def peer(distance):
        return {"seq": 2 * lax.rem(chip + distance, chips) + core}

    def z_peer(distance):
        return {"head": lax.rem(z + distance, heads)}

    def remote(source, target, sems, device):
        return pltpu.make_async_remote_copy(
            src_ref=source, dst_ref=target, send_sem=sems[0], recv_sem=sems[1],
            device_id=device, device_id_type=MESH,
        )

    barrier = pltpu.get_barrier_semaphore()
    greeted = [partner] + [peer(k) for k in range(1, chips)] + [z_peer(k) for k in range(1, heads)]
    for device in greeted:
        pl.semaphore_signal(barrier, inc=1, device_id=device, device_id_type=MESH)
    pl.semaphore_wait(barrier, len(greeted))

    core_rows = pl.ds(pl.multiple_of(core * half, 16), half)

    def weight_copy(k):
        dest = lax.rem(z + k, heads)
        return remote(
            out_weight.at[core_rows, pl.ds(pl.multiple_of(dest * width, 128), width)],
            columns.at[z, core_rows],
            (sem_w.at[0, k], sem_w.at[1, k]),
            z_peer(k),
        )

    def weight_share(k):
        block = columns.at[lax.rem(z + heads - k, heads), core_rows]
        return remote(block, block, (sem_x.at[0, k], sem_x.at[1, k]), partner)

    for k in sorted(range(1, heads), key=lambda k: -abs(k - heads / 2)):
        weight_copy(k).start()

    def copy_a(m):
        return remote(send_a.at[m, 1 - core], recv_a.at[m], (sem_a.at[0, m], sem_a.at[1, m]), partner)

    def copy_b(m, k):
        return remote(
            send_b.at[m, lax.rem(chip + k, chips)], recv_b.at[m, k - 1],
            (sem_b.at[0, m, k], sem_b.at[1, m, k]), peer(k),
        )

    def copy_c(m, k):
        block = full.at[m, core, chip]
        return remote(block, block, (sem_c.at[0, m, k], sem_c.at[1, m, k]), peer(k))

    def copy_d(m):
        return remote(full.at[m, core], full.at[m, core], (sem_d.at[0, m], sem_d.at[1, m]), partner)

    def start_a(m):
        for index in range(shards):
            send_a[m, index % 2, index // 2] = wide[index * grad_rows:(index + 1) * grad_rows, :].astype(BF16)
        copy_a(m).start()

    def step_b(m):
        copy_a(m).wait_recv()
        send_b[m] = (send_a[m, core].astype(F32) + recv_a[m].astype(F32)).astype(BF16)
        for k in range(1, chips):
            copy_b(m, k).start()

    def step_c(m):
        for k in range(1, chips):
            copy_b(m, k).wait_recv()
        total = send_b[m, chip].astype(F32)
        for k in range(1, chips):
            total = total + recv_b[m, k - 1].astype(F32)
        full[m, core, chip] = total.astype(BF16)
        for k in range(1, chips):
            copy_c(m, k).start()

    def step_d(m):
        for k in range(1, chips):
            copy_c(m, k).wait_recv()
        copy_d(m).start()

    def step_e(m):
        copy_d(m).wait_recv()

    @pl.loop(0, rows // tile)
    def _(index):
        at = pl.ds(pl.multiple_of(index * tile, tile), tile)
        k = keys[at, :]
        first_pre = dot(k, first[...])
        third_pre = dot(k, third[...])
        sig = jax.nn.sigmoid(first_pre)
        swish = first_pre * sig
        hidden_s[at, :] = (swish * third_pre).astype(BF16)
        swish_s[at, :] = swish
        gate_s[at, :] = third_pre * sig * (1.0 + first_pre * (1.0 - sig))
        weighted_s[at, :] = (values[at, :].astype(F32) * scaling[at, :]).astype(BF16)

    wide[...] = dot(hidden_s[...], weighted_s[...], ((0,), (0,)))
    start_a(0)

    @pl.loop(0, rows // tile)
    def _(index):
        at = pl.ds(pl.multiple_of(index * tile, tile), tile)
        back = dot(weighted_s[at, :], second[...], ((1,), (1,)))
        back_third_s[at, :] = (back * swish_s[at, :]).astype(BF16)
        back_first_s[at, :] = (back * gate_s[at, :]).astype(BF16)

    wide[...] = dot(keys[...], back_third_s[...], ((0,), (0,)))
    start_a(1)
    step_b(0)
    wide[...] = dot(keys[...], back_first_s[...], ((0,), (0,)))
    start_a(2)
    step_b(1)
    step_c(0)
    step_b(2)
    step_c(1)
    step_d(0)
    step_e(0)

    def renew(weight, slot):
        old = weight[...].astype(F32)
        fresh = old + step_size * current[...].astype(F32)
        ratio = jnp.sqrt(jnp.mean(old * old, axis=0, keepdims=True) + 1e-06) / jnp.sqrt(
            jnp.mean(fresh * fresh, axis=0, keepdims=True) + 1e-06
        )
        fresh_w[slot] = (fresh * ratio).astype(BF16)

    @pl.loop(0, 3 * NS_ITERS)
    def _(t):
        @pl.when(t == 1)
        def _():
            step_c(2)

        @pl.when(t == 2)
        def _():
            step_d(1)

        @pl.when(t == NS_ITERS)
        def _():
            step_e(1)

        @pl.when(t == NS_ITERS + 1)
        def _():
            step_d(2)

        @pl.when(t == 2 * NS_ITERS)
        def _():
            step_e(2)

        @pl.when(t == 2 * NS_ITERS + 1)
        def _():
            for k in range(1, heads):
                weight_copy(k).wait_recv()
                weight_share(k).start()

        @pl.when(lax.rem(t, NS_ITERS) == 0)
        def _():
            m = t // NS_ITERS
            for index in range(shards):
                wide[index * grad_rows:(index + 1) * grad_rows, :] = full[m, index % 2, index // 2].astype(F32)
            gradient = wide[...]
            square = jnp.sum(jnp.sum(gradient * gradient, axis=0, keepdims=True), axis=1, keepdims=True)
            current[...] = (gradient / (jnp.sqrt(square) + 1e-06)).astype(BF16)

        gram_wide = dot(current[...], current[...], ((1,), (1,)))
        wide[...] = gram_wide
        gram_s[...] = gram_wide.astype(BF16)
        poly_s[...] = (coef_b * wide[...] + coef_c * dot(gram_s[...], gram_s[...])).astype(BF16)
        current[...] = (coef_a * current[...].astype(F32) + dot(poly_s[...], current[...])).astype(BF16)

        @pl.when(t == NS_ITERS - 1)
        def _():
            renew(second, 2)

        @pl.when(t == 2 * NS_ITERS - 1)
        def _():
            renew(third, 1)

        @pl.when(t == 3 * NS_ITERS - 1)
        def _():
            renew(first, 0)

    @pl.loop(0, tokens // tile)
    def _(index):
        at = pl.ds(pl.multiple_of(index * tile, tile), tile)
        q = queries[at, :]
        first_pre = dot(q, fresh_w[0])
        third_pre = dot(q, fresh_w[1])
        hidden = (first_pre * jax.nn.sigmoid(first_pre) * third_pre).astype(BF16)
        head_out[at, :] = (dot(hidden, fresh_w[2]) * live_query[at, :]).astype(BF16)

    gather_half = head_out.at[pl.ds(0, part)]
    last = heads - 1
    sides = {
        "right": (z, z + 1, ag_right, rs_right, rs_send_right, 0),
        "left": (last - z, z - 1, ag_left, rs_left, rs_send_left, 1),
    }

    def ag_copy(side, k):
        place, neighbour, slots, _, _, d = sides[side]
        source = gather_half if k == 1 else slots.at[k - 2]
        return remote(source, slots.at[k - 1], (sem_ag.at[0, d, k], sem_ag.at[1, d, k]), {"head": neighbour})

    def rs_copy(side, k):
        place, neighbour, _, slots, sends, d = sides[side]
        return remote(sends.at[k - 1], slots.at[k - 1], (sem_rs.at[0, d, k], sem_rs.at[1, d, k]), {"head": neighbour})

    def projected(dest):
        cols = pl.ds(pl.multiple_of(dest * width, 128), width)
        return dot(head_out[part:, :], out_weight[:, cols])

    def round_sends(side, k):
        place, _, _, slots, sends, _ = sides[side]

        @pl.when((place <= k - 1) & (place < last))
        def _():
            dest = heads - k + z if side == "right" else k + z - heads
            mine = projected(dest)
            if k == 1:
                sends[0] = mine.astype(BF16)
            else:
                @pl.when(place == 0)
                def _():
                    sends[k - 1] = mine.astype(BF16)

                @pl.when(place >= 1)
                def _():
                    rs_copy(side, k - 1).wait_recv()
                    sends[k - 1] = (mine + slots[k - 2].astype(F32)).astype(BF16)

            rs_copy(side, k).start()

        @pl.when(place >= k - 1)
        def _():
            if k > 1:
                ag_copy(side, k - 1).wait_recv()

            @pl.when(place < last)
            def _():
                ag_copy(side, k).start()

    def gathered(side, k):
        place, _, slots, _, _, _ = sides[side]

        @pl.when(place >= k)
        def _():
            origin = z - k if side == "right" else z + k
            total_ag[...] += dot(slots[k - 1], columns[origin])

    for k in range(1, heads):
        @pl.when(2 * z < heads)
        def _():
            round_sends("left", k)
            round_sends("right", k)

        @pl.when(2 * z >= heads)
        def _():
            round_sends("right", k)
            round_sends("left", k)

        if k == 1:
            own = pl.ds(pl.multiple_of(z * width, 128), width)
            total_ag[...] = dot(head_out[:part, :], out_weight[:, own])
            wide[:part, :] = projected(z)
            for j in range(1, heads):
                weight_share(j).wait_recv()
        else:
            gathered("left", k - 1)
            gathered("right", k - 1)

    for side in ("left", "right"):
        place, _, ag_slots, rs_slots, _, _ = sides[side]

        @pl.when(place >= last)
        def _():
            ag_copy(side, last).wait_recv()

        gathered(side, last)

        @pl.when(place >= 1)
        def _():
            rs_copy(side, last).wait_recv()
            wide[:part, :] += rs_slots[last - 1].astype(F32)

    mixed[:part, :] = total_ag[...].astype(BF16)
    mixed[part:, :] = wide[:part, :].astype(BF16)

    for m in range(3):
        copy_a(m).wait_send()
        copy_d(m).wait_send()
        for k in range(1, chips):
            copy_b(m, k).wait_send()
            copy_c(m, k).wait_send()
    for k in range(1, heads):
        weight_copy(k).wait_send()
        weight_share(k).wait_send()
        for side in ("left", "right"):
            place = sides[side][0]

            @pl.when((place <= k - 1) & (place < last))
            def _():
                rs_copy(side, k).wait_send()

            @pl.when((place >= k - 1) & (place < last))
            def _():
                ag_copy(side, k).wait_send()


def on_device(
    heads, shards,
    keys, values, step_rates, queries, first_weight, third_weight, second_weight, out_weight, live_counts,
):
    groups, rows, width = keys.shape
    chips = shards // 2
    grad_rows = width // shards
    part = rows // 2
    positions = jnp.arange(rows, dtype=jnp.int32)
    live = (positions[None, :] < live_counts).astype(F32)
    scaling = (live[:groups] * step_rates[:, 0]).reshape(groups * rows, 1)
    live_query = live[groups].reshape(rows, 1)
    every = groups * rows
    vmem = pl.BlockSpec(memory_space=pltpu.VMEM)
    dma = pltpu.SemaphoreType.DMA
    return pl.pallas_call(
        functools.partial(kernel, heads, shards, 256),
        out_shape=jax.ShapeDtypeStruct((rows, width), BF16),
        in_specs=[vmem] * 9,
        out_specs=vmem,
        scratch_shapes=[
            pltpu.VMEM((every, width), F32),
            pltpu.VMEM((every, width), F32),
            pltpu.VMEM((every, width), BF16),
            pltpu.VMEM((every, width), BF16),
            pltpu.VMEM((every, width), BF16),
            pltpu.VMEM((every, width), BF16),
            pltpu.VMEM((width, width), F32),
            pltpu.VMEM((width, width), BF16),
            pltpu.VMEM((width, width), BF16),
            pltpu.VMEM((width, width), BF16),
            pltpu.VMEM((3, width, width), BF16),
            pltpu.VMEM((3, 2, chips, grad_rows, width), BF16),
            pltpu.VMEM((3, chips, grad_rows, width), BF16),
            pltpu.VMEM((3, chips, grad_rows, width), BF16),
            pltpu.VMEM((3, chips - 1, grad_rows, width), BF16),
            pltpu.VMEM((3, 2, chips, grad_rows, width), BF16),
            pltpu.VMEM((heads, width, width), BF16),
            pltpu.VMEM((rows, width), BF16),
        ]
        + [pltpu.VMEM((heads - 1, part, width), BF16)] * 6
        + [
            pltpu.VMEM((part, width), F32),
            dma((2, 3)),
            dma((2, 3, chips)),
            dma((2, 3, chips)),
            dma((2, 3)),
            dma((2, heads)),
            dma((2, heads)),
            dma((2, 2, heads)),
            dma((2, 2, heads)),
        ],
        compiler_params=pltpu.CompilerParams(
            collective_id=0, has_side_effects=True, vmem_limit_bytes=67000000
        ),
        name="fast_weight_layer",
    )(
        keys.reshape(every, width), values.reshape(every, width), scaling, queries, live_query,
        first_weight[0], third_weight[0], second_weight[0], out_weight,
    )


def solution(mesh):
    in_specs = (
        P(None, "seq", "head"),
        P(None, "seq", "head"),
        P(None, "head", "seq"),
        P("seq", "head"),
        P("head", None, None),
        P("head", None, None),
        P("head", None, None),
        P("head", None),
        P(None, "seq"),
    )
    return jax.shard_map(
        functools.partial(on_device, mesh.shape["head"], mesh.shape["seq"]),
        mesh=mesh, in_specs=in_specs, out_specs=P("seq", "head"), check_vma=False,
    )
```

time: 266 us -> 104 us (0.39)
  waiting for transfers between devices: 125 us -> 0 us
  Pallas kernels: 0 us -> 98.8 us
  matrix products: 95.3 us -> 0 us
  between operations: 15.8 us -> 0.01 us
  local copies, waits for them, and re-layouts: 17.2 us -> 3.87 us
  starting transfers between devices: 6.37 us -> 0 us
  other arithmetic: 6.05 us -> 1.41 us
    pallas_call x0 -> x1, Pallas kernels: none -> 98.8 us  [on_device(): pl.pallas_call(functools.partial(kernel, heads, shards, 256), out_shape=j...]
    dot_general x33 -> x0, matrix products: 95.3 us -> none  [the longest x9 45.8 us: poly_step(): jnp.dot(poly, current, preferred_element_type=jnp.float32)]
    psum x1 -> x0, waiting for transfers between devices: 75.4 us -> none  [on_device(): totals = lax.psum(totals, 'seq')]
    all_gather x1 -> x0, waiting for transfers between devices: 49.1 us -> none  [on_device(): lax.all_gather(head_out, 'head', axis=1, tiled=True)]
    unnamed x34 -> x3, local copies, waits for them, and re-layouts: 10.9 us -> 3.01 us
    all_to_all x1 -> x0, starting transfers between devices: 6.36 us -> none  [on_device(): lax.all_to_all(out_weight, 'head', split_axis=1, concat_axis=0, tiled=True)]
    all_to_all x1 -> x0, local copies, waits for them, and re-layouts: 5.66 us -> none  [on_device(): lax.all_to_all(out_weight, 'head', split_axis=1, concat_axis=0, tiled=True)]
    reduce_sum x2 -> x0, other arithmetic: 4.11 us -> none  [orthogonal(): scale = jnp.sqrt(jnp.sum(gradient * gradient)) + 1e-06]
  transfers between devices with their start and end apart: 3 -> 0, of which waited for: 2 -> 0; matrix products, arithmetic and copies ran while one was open for 36% -> 0% of each run, Pallas kernels for 0% -> 0%
where the time goes in v1:
time: 104 us
  Pallas kernels  98.8 us (95%)
  local copies, waits for them, and re-layouts  3.87 us (4%)
  other arithmetic  1.41 us (1%)
    pallas_call x1, Pallas kernels, on_device(): pl.pallas_call(functools.partial(kernel, heads, shards, 256), out_shape=j...  98.8 us
    unnamed x3, local copies, waits for them, and re-layouts  3.01 us

profile of v1, /device:TPU:0, one launch (start us, length us, event | category | flops | bytes accessed | tf_op | source)
XLA Modules:
  0.0 104.1 jit_solution(6988855172750200178)
XLA Ops:
  0.0 0.7 fusion
  0.7 0.7 fusion.1
  1.4 0.9 copy.11.live_query
  2.3 1.0 copy.14
  3.3 98.8 %fast_weight_layer.1 = bf16[512,640]{1,0:T(8,128)(2,1)} custom-call(bf16[1024,640]{1,0:T(8,128)(2,1)} %bitcast.16, bf16[1024,640]{1,0:T(8,128)(2,1)} %bitcast.17, f32[1024,1]{1,0:T(8,128)} %bitcast.15, bf16[512,640]{1,0:T(8,128)(2,1)} %queries.1, f32[512,1]{1,0:T(8,128)} %copy.11.live_query, bf16[640,640]{1,0:T(8,128)(2,1)} %bitcast.18, ...), custom_call_target="tpu_custom_call" | custom-call | tf_op jit(solution)/shard_map/fast_weight_layer/pallas_call | solution.py:367
  102.2 2.0 %copy.17 = bf16[512,640]{1,0:T(8,128)(2,1)} copy(bf16[512,640]{1,0:T(8,128)(2,1)} %fast_weight_layer.1) | data formatting | bytes 1310720
  (2 shorter events, 0.0 us)

commit v2 on v1

--- a/solution.py
+++ b/solution.py
@@ -24,16 +24,19 @@
 
 def kernel(
     heads, shards, tile,
-    keys, values, scaling, queries, live_query, first, third, second, out_weight,
+    keys_in, values_in, rates, queries_in, first_in, third_in, second_in, weight_in, counts,
     mixed,
+    keys, values, queries, first, third, second, out_weight, scaling,
     gate_s, swish_s, hidden_s, weighted_s, back_first_s, back_third_s,
     wide, gram_s, current, poly_s, fresh_w,
     send_a, recv_a, send_b, recv_b, full, columns, head_out,
     ag_right, ag_left, rs_right, rs_left, rs_send_right, rs_send_left, total_ag,
     sem_a, sem_b, sem_c, sem_d, sem_w, sem_x, sem_ag, sem_rs,
+    sem_in, sem_tile,
 ):
     chips = shards // 2
     rows, width = keys.shape
+    groups, group_rows = rates.shape
     grad_rows = width // shards
     z = lax.axis_index("head")
     s = lax.axis_index("seq")
@@ -56,6 +59,25 @@
             device_id=device, device_id_type=MESH,
         )
 
+    def tile_copy(index, which):
+        at = pl.ds(pl.multiple_of(index * tile, tile), tile)
+        source, target = ((keys_in, keys), (values_in, values))[which]
+        return pltpu.make_async_copy(source.at[at], target.at[at], sem_tile.at[which, index])
+
+    def input_copy(index):
+        source, target = (
+            (first_in, first), (third_in, third), (second_in, second), (queries_in, queries), (weight_in, out_weight),
+        )[index]
+        return pltpu.make_async_copy(source, target, sem_in.at[index])
+
+    input_copy(0).start()
+    input_copy(1).start()
+    for index in range(rows // tile):
+        tile_copy(index, 0).start()
+        tile_copy(index, 1).start()
+    for index in range(2, 5):
+        input_copy(index).start()
+
     barrier = pltpu.get_barrier_semaphore()
     greeted = [partner] + [peer(k) for k in range(1, chips)] + [z_peer(k) for k in range(1, heads)]
     for device in greeted:
@@ -67,7 +89,7 @@
     def weight_copy(k):
         dest = lax.rem(z + k, heads)
         return remote(
-            out_weight.at[core_rows, pl.ds(pl.multiple_of(dest * width, 128), width)],
+            weight_in.at[core_rows, pl.ds(pl.multiple_of(dest * width, 128), width)],
             columns.at[z, core_rows],
             (sem_w.at[0, k], sem_w.at[1, k]),
             z_peer(k),
@@ -83,18 +105,22 @@
     def copy_a(m):
         return remote(send_a.at[m, 1 - core], recv_a.at[m], (sem_a.at[0, m], sem_a.at[1, m]), partner)
 
-    def copy_b(m, k):
+    cut = (grad_rows // 2 + 15) // 16 * 16
+    pieces = (pl.ds(0, cut), pl.ds(cut, grad_rows - cut))
+
+    def copy_b(m, k, p):
         return remote(
-            send_b.at[m, lax.rem(chip + k, chips)], recv_b.at[m, k - 1],
-            (sem_b.at[0, m, k], sem_b.at[1, m, k]), peer(k),
+            send_b.at[m, lax.rem(chip + k, chips), pieces[p]], recv_b.at[m, k - 1, pieces[p]],
+            (sem_b.at[0, m, k, p], sem_b.at[1, m, k, p]), peer(k),
         )
 
-    def copy_c(m, k):
-        block = full.at[m, core, chip]
-        return remote(block, block, (sem_c.at[0, m, k], sem_c.at[1, m, k]), peer(k))
-
-    def copy_d(m):
-        return remote(full.at[m, core], full.at[m, core], (sem_d.at[0, m], sem_d.at[1, m]), partner)
+    def copy_c(m, k, p):
+        block = full.at[m, core, chip, pieces[p]]
+        return remote(block, block, (sem_c.at[0, m, k, p], sem_c.at[1, m, k, p]), peer(k))
+
+    def copy_d(m, p):
+        block = full.at[m, core, :, pieces[p]]
+        return remote(block, block, (sem_d.at[0, m, p], sem_d.at[1, m, p]), partner)
 
     def start_a(m):
         for index in range(shards):
@@ -104,30 +130,43 @@
     def step_b(m):
         copy_a(m).wait_recv()
         send_b[m] = (send_a[m, core].astype(F32) + recv_a[m].astype(F32)).astype(BF16)
-        for k in range(1, chips):
-            copy_b(m, k).start()
+        for p in range(2):
+            for k in range(1, chips):
+                copy_b(m, k, p).start()
 
     def step_c(m):
-        for k in range(1, chips):
-            copy_b(m, k).wait_recv()
-        total = send_b[m, chip].astype(F32)
-        for k in range(1, chips):
-            total = total + recv_b[m, k - 1].astype(F32)
-        full[m, core, chip] = total.astype(BF16)
-        for k in range(1, chips):
-            copy_c(m, k).start()
+        for p in range(2):
+            for k in range(1, chips):
+                copy_b(m, k, p).wait_recv()
+            total = send_b[m, chip, pieces[p]].astype(F32)
+            for k in range(1, chips):
+                total = total + recv_b[m, k - 1, pieces[p]].astype(F32)
+            full[m, core, chip, pieces[p]] = total.astype(BF16)
+            for k in range(1, chips):
+                copy_c(m, k, p).start()
 
     def step_d(m):
-        for k in range(1, chips):
-            copy_c(m, k).wait_recv()
-        copy_d(m).start()
+        for p in range(2):
+            for k in range(1, chips):
+                copy_c(m, k, p).wait_recv()
+            copy_d(m, p).start()
 
     def step_e(m):
-        copy_d(m).wait_recv()
+        for p in range(2):
+            copy_d(m, p).wait_recv()
+
+    for group in range(groups):
+        rate = jnp.broadcast_to(rates[group:group + 1, :], (128, group_rows)).T
+        place = lax.broadcasted_iota(jnp.int32, (group_rows, 128), 0)
+        scaling[group * group_rows:(group + 1) * group_rows, :] = jnp.where(place < counts[group, 0], rate, 0.0)
+
+    input_copy(0).wait()
+    input_copy(1).wait()
 
     @pl.loop(0, rows // tile)
     def _(index):
         at = pl.ds(pl.multiple_of(index * tile, tile), tile)
+        tile_copy(index, 0).wait()
         k = keys[at, :]
         first_pre = dot(k, first[...])
         third_pre = dot(k, third[...])
@@ -136,10 +175,13 @@
         hidden_s[at, :] = (swish * third_pre).astype(BF16)
         swish_s[at, :] = swish
         gate_s[at, :] = third_pre * sig * (1.0 + first_pre * (1.0 - sig))
-        weighted_s[at, :] = (values[at, :].astype(F32) * scaling[at, :]).astype(BF16)
+        tile_copy(index, 1).wait()
+        scale = jnp.concatenate([scaling[at, :]] * (width // 128), axis=1)
+        weighted_s[at, :] = (values[at, :].astype(F32) * scale).astype(BF16)
 
     wide[...] = dot(hidden_s[...], weighted_s[...], ((0,), (0,)))
     start_a(0)
+    input_copy(2).wait()
 
     @pl.loop(0, rows // tile)
     def _(index):
@@ -148,15 +190,13 @@
         back_third_s[at, :] = (back * swish_s[at, :]).astype(BF16)
         back_first_s[at, :] = (back * gate_s[at, :]).astype(BF16)
 
+    step_b(0)
     wide[...] = dot(keys[...], back_third_s[...], ((0,), (0,)))
     start_a(1)
-    step_b(0)
     wide[...] = dot(keys[...], back_first_s[...], ((0,), (0,)))
     start_a(2)
+    step_c(0)
     step_b(1)
-    step_c(0)
-    step_b(2)
-    step_c(1)
     step_d(0)
     step_e(0)
 
@@ -170,21 +210,9 @@
 
     @pl.loop(0, 3 * NS_ITERS)
     def _(t):
-        @pl.when(t == 1)
-        def _():
-            step_c(2)
-
-        @pl.when(t == 2)
-        def _():
-            step_d(1)
-
         @pl.when(t == NS_ITERS)
         def _():
             step_e(1)
-
-        @pl.when(t == NS_ITERS + 1)
-        def _():
-            step_d(2)
 
         @pl.when(t == 2 * NS_ITERS)
         def _():
@@ -209,6 +237,24 @@
         wide[...] = gram_wide
         gram_s[...] = gram_wide.astype(BF16)
         poly_s[...] = (coef_b * wide[...] + coef_c * dot(gram_s[...], gram_s[...])).astype(BF16)
+
+        @pl.when(t == 0)
+        def _():
+            step_c(1)
+            step_b(2)
+
+        @pl.when(t == NS_ITERS - 1)
+        def _():
+            step_d(1)
+
+        @pl.when(t == NS_ITERS)
+        def _():
+            step_c(2)
+
+        @pl.when(t == 2 * NS_ITERS - 1)
+        def _():
+            step_d(2)
+
         current[...] = (coef_a * current[...].astype(F32) + dot(poly_s[...], current[...])).astype(BF16)
 
         @pl.when(t == NS_ITERS - 1)
@@ -222,15 +268,6 @@
         @pl.when(t == 3 * NS_ITERS - 1)
         def _():
             renew(first, 0)
-
-    @pl.loop(0, tokens // tile)
-    def _(index):
-        at = pl.ds(pl.multiple_of(index * tile, tile), tile)
-        q = queries[at, :]
-        first_pre = dot(q, fresh_w[0])
-        third_pre = dot(q, fresh_w[1])
-        hidden = (first_pre * jax.nn.sigmoid(first_pre) * third_pre).astype(BF16)
-        head_out[at, :] = (dot(hidden, fresh_w[2]) * live_query[at, :]).astype(BF16)
 
     gather_half = head_out.at[pl.ds(0, part)]
     last = heads - 1
@@ -252,7 +289,7 @@
         cols = pl.ds(pl.multiple_of(dest * width, 128), width)
         return dot(head_out[part:, :], out_weight[:, cols])
 
-    def round_sends(side, k):
+    def sums_out(side, k):
         place, _, _, slots, sends, _ = sides[side]
 
         @pl.when((place <= k - 1) & (place < last))
@@ -273,6 +310,9 @@
 
             rs_copy(side, k).start()
 
+    def gather_out(side, k):
+        place = sides[side][0]
+
         @pl.when(place >= k - 1)
         def _():
             if k > 1:
@@ -282,6 +322,10 @@
             def _():
                 ag_copy(side, k).start()
 
+    def round_sends(side, k):
+        sums_out(side, k)
+        gather_out(side, k)
+
     def gathered(side, k):
         place, _, slots, _, _, _ = sides[side]
 
@@ -290,7 +334,38 @@
             origin = z - k if side == "right" else z + k
             total_ag[...] += dot(slots[k - 1], columns[origin])
 
-    for k in range(1, heads):
+    input_copy(3).wait()
+    input_copy(4).wait()
+    at_end = jnp.where((z == 0) | (z == last), 1, 0)
+
+    @pl.loop(0, 2)
+    def _(turn):
+        index = lax.rem(turn + at_end, 2)
+        at = pl.ds(pl.multiple_of(index * part, part), part)
+        q = queries[at, :]
+        first_pre = dot(q, fresh_w[0])
+        third_pre = dot(q, fresh_w[1])
+        hidden = (first_pre * jax.nn.sigmoid(first_pre) * third_pre).astype(BF16)
+        place = lax.broadcasted_iota(jnp.int32, (part, width), 0) + index * part
+        head_out[at, :] = jnp.where(place < counts[groups, 0], dot(hidden, fresh_w[2]), 0.0).astype(BF16)
+
+        @pl.when(index == 1)
+        def _():
+            sums_out("left", 1)
+            sums_out("right", 1)
+
+        @pl.when(index == 0)
+        def _():
+            gather_out("left", 1)
+            gather_out("right", 1)
+
+    own = pl.ds(pl.multiple_of(z * width, 128), width)
+    total_ag[...] = dot(head_out[:part, :], out_weight[:, own])
+    wide[:part, :] = projected(z)
+    for j in range(1, heads):
+        weight_share(j).wait_recv()
+
+    for k in range(2, heads):
         @pl.when(2 * z < heads)
         def _():
             round_sends("left", k)
@@ -301,15 +376,8 @@
             round_sends("right", k)
             round_sends("left", k)
 
-        if k == 1:
-            own = pl.ds(pl.multiple_of(z * width, 128), width)
-            total_ag[...] = dot(head_out[:part, :], out_weight[:, own])
-            wide[:part, :] = projected(z)
-            for j in range(1, heads):
-                weight_share(j).wait_recv()
-        else:
-            gathered("left", k - 1)
-            gathered("right", k - 1)
+        gathered("left", k - 1)
+        gathered("right", k - 1)
 
     for side in ("left", "right"):
         place, _, ag_slots, rs_slots, _, _ = sides[side]
@@ -330,10 +398,11 @@
 
     for m in range(3):
         copy_a(m).wait_send()
-        copy_d(m).wait_send()
-        for k in range(1, chips):
-            copy_b(m, k).wait_send()
-            copy_c(m, k).wait_send()
+        for p in range(2):
+            copy_d(m, p).wait_send()
+            for k in range(1, chips):
+                copy_b(m, k, p).wait_send()
+                copy_c(m, k, p).wait_send()
     for k in range(1, heads):
         weight_copy(k).wait_send()
         weight_share(k).wait_send()
@@ -357,19 +426,25 @@
     chips = shards // 2
     grad_rows = width // shards
     part = rows // 2
-    positions = jnp.arange(rows, dtype=jnp.int32)
-    live = (positions[None, :] < live_counts).astype(F32)
-    scaling = (live[:groups] * step_rates[:, 0]).reshape(groups * rows, 1)
-    live_query = live[groups].reshape(rows, 1)
     every = groups * rows
+    tile = 256
     vmem = pl.BlockSpec(memory_space=pltpu.VMEM)
+    hbm = pl.BlockSpec(memory_space=pl.ANY)
     dma = pltpu.SemaphoreType.DMA
     return pl.pallas_call(
-        functools.partial(kernel, heads, shards, 256),
+        functools.partial(kernel, heads, shards, tile),
         out_shape=jax.ShapeDtypeStruct((rows, width), BF16),
-        in_specs=[vmem] * 9,
+        in_specs=[hbm, hbm, vmem, hbm, hbm, hbm, hbm, hbm, pl.BlockSpec(memory_space=pltpu.SMEM)],
         out_specs=vmem,
         scratch_shapes=[
+            pltpu.VMEM((every, width), BF16),
+            pltpu.VMEM((every, width), BF16),
+            pltpu.VMEM((rows, width), BF16),
+            pltpu.VMEM((width, width), BF16),
+            pltpu.VMEM((width, width), BF16),
+            pltpu.VMEM((width, width), BF16),
+            pltpu.VMEM(out_weight.shape, BF16),
+            pltpu.VMEM((every, 128), F32),
             pltpu.VMEM((every, width), F32),
             pltpu.VMEM((every, width), F32),
             pltpu.VMEM((every, width), BF16),
@@ -393,21 +468,23 @@
         + [
             pltpu.VMEM((part, width), F32),
             dma((2, 3)),
-            dma((2, 3, chips)),
-            dma((2, 3, chips)),
-            dma((2, 3)),
+            dma((2, 3, chips, 2)),
+            dma((2, 3, chips, 2)),
+            dma((2, 3, 2)),
             dma((2, heads)),
             dma((2, heads)),
             dma((2, 2, heads)),
             dma((2, 2, heads)),
+            dma((5,)),
+            dma((2, every // tile)),
         ],
         compiler_params=pltpu.CompilerParams(
             collective_id=0, has_side_effects=True, vmem_limit_bytes=67000000
         ),
         name="fast_weight_layer",
     )(
-        keys.reshape(every, width), values.reshape(every, width), scaling, queries, live_query,
-        first_weight[0], third_weight[0], second_weight[0], out_weight,
+        keys.reshape(every, width), values.reshape(every, width), step_rates[:, 0], queries,
+        first_weight[0], third_weight[0], second_weight[0], out_weight, live_counts,
     )
 
 

time: 104 us -> 100 us (0.962)
  Pallas kernels: 98.8 us -> 95.5 us
  other arithmetic: 1.41 us -> 0 us
    pallas_call x1, Pallas kernels: 98.8 us -> 95.5 us  [on_device(): pl.pallas_call(functools.partial(kernel, heads, shards, tile), out_shape=...]
    unnamed x3, local copies, waits for them, and re-layouts: 3.01 us -> 4.54 us
where the time goes in v2:
time: 100 us
  Pallas kernels  95.5 us (96%)
  local copies, waits for them, and re-layouts  4.54 us (5%)
    pallas_call x1, Pallas kernels, on_device(): pl.pallas_call(functools.partial(kernel, heads, shards, tile), out_shape=...  95.5 us
    unnamed x3, local copies, waits for them, and re-layouts  4.54 us

profile of v2, /device:TPU:0, one launch (start us, length us, event | category | flops | bytes accessed | tf_op | source)
XLA Modules:
  0.0 100.0 jit_solution(7552202163439100241)
XLA Ops:
  0.0 1.3 %copy.10.counts = s32[3,1]{1,0:T(4,128)} copy(s32[3,1]{0,1:T(1,128)} %param.17) | data formatting | bytes 24 | tf_op args[8]
  1.3 1.3 %copy.13 = f32[2,1,512]{2,0,1:T(2,128)} copy(f32[2,1,512]{2,1,0:T(1,128)} %param.11) | data formatting | bytes 8192
  2.6 95.5 %fast_weight_layer.1 = bf16[512,640]{1,0:T(8,128)(2,1)} custom-call(bf16[1024,640]{1,0:T(8,128)(2,1)} %bitcast.8, bf16[1024,640]{1,0:T(8,128)(2,1)} %bitcast.9, f32[2,512]{1,0:T(2,128)} %bitcast.13, bf16[512,640]{1,0:T(8,128)(2,1)} %queries_in.1, bf16[640,640]{1,0:T(8,128)(2,1)} %bitcast.10, bf16[640,640]{1,0:T(8,128)(2,1)} %bitcast.11, ...), custom_call_target="tpu_custom_call" | custom-call | tf_op jit(solution)/shard_map/fast_weight_layer/pallas_call | solution.py:434
  98.0 2.0 %copy.15 = bf16[512,640]{1,0:T(8,128)(2,1)} copy(bf16[512,640]{1,0:T(8,128)(2,1)} %fast_weight_layer.1) | data formatting | bytes 1310720
